TPU v7x, 256 devices: a whole 4x4x8 slice. The times are simulated.
256 devices in a mesh: seq: 8 (over y, core), exp: 32 (over z, x).
Axes of the slice: x: 4, y: 4, z: 8, core: 2. Of those that a mesh axis runs over, the one named last changes fastest.
Arguments:
- query_rows: bfloat16 [4096, 4096], P('seq', 'exp'), may hold values from -6 to 6
- key_rows: bfloat16 [4096, 4096], P('seq', 'exp'), may hold values from -6 to 6
- value_rows: bfloat16 [4096, 4096], P('seq', 'exp'), may hold values from -6 to 6
- output_gate: bfloat16 [4096, 4096], P('seq', 'exp'), may hold values from -6 to 6
- log_decay: float32 [32, 4096], P('exp', 'seq'), may hold values from -0.8 to 0
- write_rate: float32 [32, 4096], P('exp', 'seq'), may hold values from 0.001 to 1
- doc_start: int32 [4096], P('seq'), may hold values from 0 to 1, as said below
- state_in: float32 [32, 128, 128], P('exp'), may hold values from -6 to 6
- head_gain: float32 [128], replicated, may hold values from 0.5 to 1.5
- out_weight: bfloat16 [4096, 2048], P('exp'), may hold values from -0.09375 to 0.09375
- residual: bfloat16 [4096, 2048], P(('seq', 'exp')), may hold values from -6 to 6
- post_gain: float32 [2048], replicated, may hold values from 0.5 to 1.5
- expert_ids: int32 [4096, 10], P(('seq', 'exp')), may hold values from 0 to 255, all different within a row; in each aligned block of 16 rows (0 to 15, 16 to 31, ...) at most 2 rows name the same one
- expert_scale: float32 [4096, 10], P(('seq', 'exp')), may hold values from 0.02 to 0.2
- w_gate_up: bfloat16 [256, 2048, 1024], P(('seq', 'exp')), may hold values from -0.125 to 0.125
- w_down: bfloat16 [256, 512, 2048], P(('seq', 'exp')), may hold values from -0.25 to 0.25
Outputs:
- layer_out: bfloat16 [4096, 2048], P(('seq', 'exp'))
Inputs may be any that keep to these rules, and one draw needn't show every extreme that they name: `doc_start`: one or two tokens after the first begin a new document. `expert_ids`: each token names 10 different experts; among the tokens of one device (aligned blocks of 512 // 32 rows) no expert is named more than 2 times, a bound that some block reaches.
All inputs are finite; a program needn't handle non-finite values.
Results may differ from a plain program's by a relative error of at most 0.014.
Values may be sent and summed in bfloat16 or wider, within the bound.
No kernel may reach another device: no remote copies, remote signals or barrier semaphores. Data moves between devices by JAX's collectives and lax.ppermute only.
A program may use at most 64 MiB of HBM per device.

v0:
```python
import jax
import jax.numpy as jnp
from jax import lax
from jax.sharding import PartitionSpec as P

DK = 128
DV = 128
FFE = 512
TOP = 10


def passed_along(array, axis, by):
    length = lax.axis_size(axis)
    pairs = [(i, i + by) for i in range(length) if 0 <= i + by < length]
    return lax.ppermute(array, axis, pairs)


def contract(form, left, right):
    return jnp.einsum(form, left, right, precision=lax.Precision.HIGHEST)


def by_blocks(rows, heads, block):
    length = rows.shape[0]
    width = rows.shape[1] // heads
    shaped = rows.astype(jnp.float32).reshape(length // block, block, heads, width)
    return shaped.transpose(2, 0, 1, 3)


def compose(earlier, later):
    return (
        contract("hkl,hlm->hkm", earlier[0], later[0]),
        contract("hvl,hlm->hvm", earlier[1], later[0]) + later[1],
    )


def local(
    query_rows,
    key_rows,
    value_rows,
    output_gate,
    log_decay,
    write_rate,
    doc_start,
    state_in,
    head_gain,
    out_weight,
    residual,
    post_gain,
    expert_ids,
    expert_scale,
    w_gate_up,
    w_down,
):
    length = query_rows.shape[0]
    heads = log_decay.shape[0]
    block = min(64, length)
    blocks = length // block
    query = by_blocks(query_rows, heads, block)
    key = by_blocks(key_rows, heads, block)
    key = key * lax.rsqrt(jnp.sum(key * key, axis=-1, keepdims=True) + 1e-06)
    value = by_blocks(value_rows, heads, block)
    decay_log = log_decay.reshape(heads, blocks, block)
    rate = write_rate.reshape(heads, blocks, block)
    resets = jnp.cumsum(doc_start.reshape(blocks, block), axis=-1)
    total_log = jnp.cumsum(decay_log, axis=-1)
    place = jnp.arange(block)
    within = place[:, None] >= place[None, :]
    strict = place[:, None] > place[None, :]
    same = (resets[:, :, None] == resets[:, None, :]) & within
    spread = total_log[..., :, None] - total_log[..., None, :]
    pair_decay = jnp.where(same, jnp.exp(jnp.where(same, spread, 0.0)), 0.0)
    start_decay = jnp.where(resets == 0, jnp.exp(total_log), 0.0)
    end_decay = jnp.where(resets == resets[:, -1:], jnp.exp(total_log[..., -1:] - total_log), 0.0)
    key_inner = contract("hbtk,hbsk->hbts", key, key)
    lower = jnp.where(strict, rate[..., :, None] * pair_decay * key_inner, 0.0)
    system = lower + jnp.eye(block, dtype=jnp.float32)
    right = jnp.concatenate(
        [rate[..., None] * value, (rate * start_decay)[..., None] * key], axis=-1
    )
    solved = lax.linalg.triangular_solve(
        system, right, left_side=True, lower=True, unit_diagonal=True
    )
    update = solved[..., :DV]
    erase = solved[..., DV:]
    tail_key = end_decay[..., None] * key
    identity = jnp.broadcast_to(jnp.eye(DK, dtype=jnp.float32), (heads, DK, DK))
    transfer = start_decay[..., -1, None, None] * identity[:, None] - contract(
        "hbtk,hbtl->hbkl", erase, tail_key
    )
    written = contract("hbtv,hbtk->hbvk", update, tail_key)
    scores = contract("hbtk,hbsk->hbts", query, key) * pair_decay

    def fold_block(carry, pair):
        return (compose(carry, pair), None)

    empty_state = jnp.zeros((heads, DV, DK), jnp.float32)
    moved_transfer = jnp.moveaxis(transfer, 1, 0)
    moved_written = jnp.moveaxis(written, 1, 0)
    (device_transfer, device_written), unused = lax.scan(
        fold_block, (identity, empty_state), (moved_transfer, moved_written)
    )
    first = lax.axis_index("seq") == 0

    def relay(turn, carry):
        sent = contract("hvk,hkl->hvl", carry, device_transfer) + device_written
        moved = passed_along(sent.astype(jnp.bfloat16), "seq", 1).astype(sent.dtype)
        return jnp.where(first, state_in, moved)

    start_state = lax.fori_loop(0, lax.axis_size("seq") - 1, relay, state_in)

    def run_block(state, pieces):
        query_now, update_now, erase_now, scores_now, start_now, transfer_now, written_now = pieces
        delta = update_now - contract("htk,hvk->htv", erase_now, state)
        output = start_now[..., None] * contract("htk,hvk->htv", query_now, state) + contract(
            "hts,hsv->htv", scores_now, delta
        )
        state = contract("hvk,hkl->hvl", state, transfer_now) + written_now
        return (state, output)

    pieces = (query, update, erase, scores, start_decay, transfer, written)
    final, outputs = lax.scan(
        run_block, start_state, tuple((jnp.moveaxis(piece, 1, 0) for piece in pieces))
    )
    head_out = jnp.moveaxis(outputs, 2, 1).reshape(length, heads, DV)
    gate = output_gate.astype(jnp.float32).reshape(length, heads, DV)
    scaled = head_out * lax.rsqrt(jnp.mean(head_out * head_out, axis=-1, keepdims=True) + 1e-06)
    gated = (
        (scaled * head_gain * jax.nn.silu(gate)).astype(jnp.bfloat16).reshape(length, heads * DV)
    )
    rows = residual.shape[0]
    width = residual.shape[1]
    attended = lax.psum_scatter(
        jnp.dot(gated, out_weight, preferred_element_type=jnp.float32).astype(jnp.bfloat16),
        "exp",
        scatter_dimension=0,
        tiled=True,
    ).astype(jnp.float32)
    stream = (residual.astype(jnp.float32) + attended).astype(jnp.bfloat16)
    wide = stream.astype(jnp.float32)
    normed = (
        wide * lax.rsqrt(jnp.mean(wide * wide, axis=-1, keepdims=True) + 1e-06) * post_gain
    ).astype(jnp.bfloat16)
    seq_count = lax.axis_size("seq")
    exp_count = lax.axis_size("exp")
    experts = seq_count * exp_count
    capacity = max(2, rows * TOP * 12 // (5 * experts))
    flat_ids = expert_ids.reshape(-1)
    hits = (flat_ids[:, None] == jnp.arange(experts, dtype=jnp.int32)[None, :]).astype(jnp.int32)
    rank = jnp.sum(jnp.cumsum(hits, axis=0) * hits, axis=1) - 1
    target = flat_ids * capacity + rank
    source_rows = jnp.repeat(normed, TOP, axis=0)
    outgoing = jnp.zeros((experts * capacity, width), jnp.bfloat16).at[target].set(source_rows)
    outgoing = outgoing.reshape(seq_count, exp_count, capacity, width)
    arrived = lax.all_to_all(
        lax.all_to_all(outgoing, "seq", split_axis=0, concat_axis=0, tiled=True),
        "exp",
        split_axis=1,
        concat_axis=1,
        tiled=True,
    )
    flat = arrived.reshape(-1, width)
    both = jnp.dot(flat, w_gate_up[0], preferred_element_type=jnp.float32)
    hidden = (jax.nn.silu(both[:, :FFE]) * both[:, FFE:]).astype(jnp.bfloat16)
    returned = lax.all_to_all(
        lax.all_to_all(
            jnp.dot(hidden, w_down[0], preferred_element_type=jnp.float32)
            .astype(jnp.bfloat16)
            .reshape(arrived.shape),
            "seq",
            split_axis=0,
            concat_axis=0,
            tiled=True,
        ),
        "exp",
        split_axis=1,
        concat_axis=1,
        tiled=True,
    )
    picked = returned.reshape(-1, width)[target].astype(jnp.float32).reshape(rows, TOP, width)
    moe = jnp.sum(expert_scale[..., None] * picked, axis=1)
    return (wide + moe).astype(jnp.bfloat16)


def solution(mesh):
    return jax.shard_map(
        local,
        mesh=mesh,
        in_specs=(
            P("seq", "exp"),
            P("seq", "exp"),
            P("seq", "exp"),
            P("seq", "exp"),
            P("exp", "seq"),
            P("exp", "seq"),
            P("seq"),
            P("exp", None, None),
            P(),
            P("exp", None),
            P(("seq", "exp"), None),
            P(),
            P(("seq", "exp"), None),
            P(("seq", "exp"), None),
            P(("seq", "exp"), None, None),
            P(("seq", "exp"), None, None),
        ),
        out_specs=P(("seq", "exp"), None),
        check_vma=False,
    )
```

profile of v0, /device:TPU:4, one launch (start us, length us, event | category | flops | bytes accessed | tf_op | source)
XLA Modules:
  0.0 599.0 jit_solution(11515922365121510422)
XLA Ops:
  14.5 39.3 %custom-call.3 = f32[1,8,1,64,64]{3,4,2,1,0:T(8,128)S(1)} custom-call(f32[1,8,1,64,64]{4,3,2,1,0:T(8,128)S(1)} %fusion.44), custom_call_target="InvertDiagBlocksLowerTriangular" | custom-call | tf_op jit(solution)/shard_map/triangular_solve | solution.py:80
  58.3 5.2 while.34
  65.7 42.1 %while.35 = (s32[]{:T(128)}, f32[1,128,128]{2,1,0:T(8,128)S(1)}, pred[]{:T(512)}, f32[1,128,128]{2,1,0:T(8,128)}, f32[1,128,128]{2,1,0:T(8,128)}, /*index=5*/f32[1,128,128]{2,1,0:T(8,128)}, s32[]{:T(128)}) while((s32[]{:T(128)}, f32[1,128,128]{2,1,0:T(8,128)S(1)}, pred[]{:T(512)}, f32[1,128,128]{2,1,0:T(8,128)}, f32[1,128,128]{2,1,0:T(8,128)}, ...), condition=%wide.region_6.7_spmd, body=%wide.region_5.6_spmd.sunk | while | flops 25231360 | bytes 524406 | solution.py:109
  77.2 3.6 collective-permute-start
  83.5 3.6 collective-permute-start
  89.9 3.6 collective-permute-start
  96.2 3.6 collective-permute-start
  102.6 3.6 collective-permute-start
  110.9 24.3 %while.36 = (s32[]{:T(128)}, f32[1,128,128]{1,2,0:T(8,128)S(1)}, f32[8,1,64,128]{3,2,1,0:T(8,128)}, f32[8,1,128,128]{3,2,1,0:T(8,128)S(1)}, f32[8,1,128,128]{2,3...) while((s32[]{:T(128)}, f32[1,128,128]{1,2,0:T(8,128)S(1)}, ...), condition=%wide.region_8.9_spmd, body=%wide.region_7.8_spmd.sunk | while | flops 56664064 | bytes 823413 | solution.py:121
  141.7 222.1 %reduce-scatter.2.cloned.1.call-done = bf16[16,2048]{1,0:T(8,128)(2,1)} async-done(((bf16[512,2048]{1,0:T(8,128)(2,1)}), bf16[16,2048]{1,0:T(8,128)(2,1)}) %reduce-scatter.2.cloned.1.call-update) | async-done | bytes 65552 | tf_op jit(solution)/shard_map/reduce_scatter | solution.py:132
  366.9 3.8 scatter_custom_fusion
  370.7 4.4 reshape.481
  375.1 31.5 %all_to_all.20 = bf16[8,32,2,2048]{3,2,1,0:T(2,128)(2,1)S(1)} all-to-all(bf16[8,32,2,2048]{3,2,1,0:T(2,128)(2,1)} %reshape.481), channel_id=1, replica_groups=mesh['seq'=8,'exp'=32] {'seq'}, dimensions={0} | all-to-all | bytes 4194304 | tf_op jit(solution)/shard_map/all_to_all | solution.py:155
  408.9 57.9 %all_to_all.21 = bf16[8,32,2,2048]{3,2,0,1:T(2,128)(2,1)S(1)} all-to-all(bf16[8,32,2,2048]{3,2,0,1:T(2,128)(2,1)S(1)} %copy.96), channel_id=1, replica_groups=mesh['seq'=8,'exp'=32] {'exp'}, dimensions={1} | all-to-all | bytes 4194304 | tf_op jit(solution)/shard_map/all_to_all | solution.py:154
  469.9 4.1 reshape.482
  474.0 5.1 fusion.34
  481.8 4.4 reshape.483
  486.2 30.7 %all_to_all.22 = bf16[8,32,2,2048]{3,2,1,0:T(2,128)(2,1)S(1)} all-to-all(bf16[8,32,2,2048]{3,2,1,0:T(2,128)(2,1)} %reshape.483), channel_id=1, replica_groups=mesh['seq'=8,'exp'=32] {'seq'}, dimensions={0} | all-to-all | bytes 4194304 | tf_op jit(solution)/shard_map/all_to_all | solution.py:165
  517.0 3.6 copy.98
  520.5 5.6 all-to-all-start.3
  526.2 49.5 %all-to-all-done.3 = bf16[8,32,2,2048]{3,2,0,1:T(2,128)(2,1)} async-done(((bf16[8,32,2,2048]{3,2,0,1:T(2,128)(2,1)}), bf16[8,32,2,2048]{3,2,0,1:T(2,128)(2,1)}, u32[]{:S(2)}, u32[]{:S(2)}) %all-to-all-start.3) | async-done | bytes 2097184 | tf_op jit(solution)/shard_map/all_to_all | solution.py:164
  575.7 4.6 copy.99
  580.3 4.1 reshape.484
  584.4 3.5 gather_fusion
  (193 shorter events, 92.1 us)
Async XLA Ops:
  6.5 472.6 %copy-start = (bf16[1,512,2048]{2,1,0:T(8,128)(2,1)S(1)}, bf16[1,512,2048]{2,1,0:T(8,128)(2,1)}, u32[]{:S(2)}) copy-start(bf16[1,512,2048]{2,1,0:T(8,128)(2,1)} %param.37) | copy-start | bytes 6291460
  6.5 47.6 %copy-start.3 = (bf16[512,128]{1,0:T(8,128)(2,1)S(1)}, bf16[512,128]{1,0:T(8,128)(2,1)}, u32[]{:S(2)}) copy-start(bf16[512,128]{1,0:T(8,128)(2,1)} %param.24) | copy-start | bytes 393220
  6.5 357.3 %reduce-scatter.2.cloned.1.call-start = ((), (), s32[]{:S(2)}) async-start(), calls=%async_computation.5 | async-start | bytes 2162688 | tf_op jit(solution)/shard_map/reduce_scatter | solution.py:132
  12.1 43.8 %copy-start.7 = (pred[64,64]{1,0:T(8,128)(4,1)}, pred[64,64]{1,0:T(8,128)(4,1)S(1)}, u32[]{:S(2)}) copy-start(pred[64,64]{1,0:T(8,128)(4,1)S(1)} %get-tuple-element.274) | copy-start | bytes 12292
  66.8 2.6 collective-permute-start
  71.3 4.0 collective-permute-start
  77.2 4.4 collective-permute-start
  83.5 4.4 collective-permute-start
  89.9 4.4 collective-permute-start
  96.2 4.4 collective-permute-start
  102.6 4.4 collective-permute-start
  110.9 25.5 %copy-start.8 = (f32[128]{0:T(128)S(1)}, f32[128]{0:T(128)}, u32[]{:S(2)}) copy-start(f32[128]{0:T(128)} %param.30) | copy-start | bytes 1540
  137.6 3.1 copy-start.4
  140.7 223.1 %copy-start.1 = (bf16[16,2048]{1,0:T(8,128)(2,1)S(1)}, bf16[16,2048]{1,0:T(8,128)(2,1)}, u32[]{:S(2)}) copy-start(bf16[16,2048]{1,0:T(8,128)(2,1)} %param.32) | copy-start | bytes 196612
  140.7 224.0 %copy-start.6 = (f32[2048]{0:T(1024)S(1)}, f32[2048]{0:T(1024)}, u32[]{:S(2)}) copy-start(f32[2048]{0:T(1024)} %param.33) | copy-start | bytes 24580
  520.5 55.2 %all-to-all-start.3 = ((bf16[8,32,2,2048]{3,2,0,1:T(2,128)(2,1)}), bf16[8,32,2,2048]{3,2,0,1:T(2,128)(2,1)}, u32[]{:S(2)}, u32[]{:S(2)}) async-start(bf16[8,32,2,2048]{3,2,0,1:T(2,128)(2,1)} %copy.98), calls=%async_computation.4 | async-start | bytes 4194304 | tf_op jit(solution)/shard_map/all_to_all | solution.py:164
  587.9 1.5 copy-start.5
  587.9 3.6 copy-start.2
Sparse Core Ops, SparseCore 0:
  140.9 222.8 reduce-scatter.1
where the time goes:
time: 602 us; the launch traced here: 599 us
  waiting for transfers between devices  278 us (46%)
  blocking collectives  120 us (20%)
  other arithmetic  59.3 us (10%)
  matrix products  52.6 us (9%)
  local copies, waits for them, and re-layouts  46.5 us (8%)
  starting transfers between devices  28.3 us (5%)
  between operations  13.7 us (2%)
    reduce_scatter x1, waiting for transfers between devices, local(): lax.psum_scatter(jnp.dot(gated, out_weight, preferred_element_type=jnp.fl...  222 us
    all_to_all x1, blocking collectives, local(): lax.all_to_all(lax.all_to_all(outgoing, 'seq', split_axis=0, concat_axis=...  57.9 us
    all_to_all x1, waiting for transfers between devices, local(): lax.all_to_all(lax.all_to_all(jnp.dot(hidden, w_down[0], preferred_elemen...  49.5 us
    dot_general x59, matrix products, contract(): return jnp.einsum(form, left, right, precision=lax.Precision.HIGHEST)  41.1 us
    another operation x4, other arithmetic, local(): lax.linalg.triangular_solve(system, right, left_side=True, lower=True, un...  39.4 us
    all_to_all x1, blocking collectives, local(): lax.all_to_all(outgoing, 'seq', split_axis=0, concat_axis=0, tiled=True)  31.5 us
    all_to_all x1, blocking collectives, local(): lax.all_to_all(jnp.dot(hidden, w_down[0], preferred_element_type=jnp.floa...  30.7 us
    ppermute x7, starting transfers between devices, passed_along(): return lax.ppermute(array, axis, pairs)  22.7 us
  transfers between devices with their start and end apart: 9, of which 9 were waited for; matrix products, arithmetic and copies ran while one was open for 0% of the time, Pallas kernels for 0%

commit v1 on v0

--- a/solution.py
+++ b/solution.py
@@ -161,20 +161,28 @@
     flat = arrived.reshape(-1, width)
     both = jnp.dot(flat, w_gate_up[0], preferred_element_type=jnp.float32)
     hidden = (jax.nn.silu(both[:, :FFE]) * both[:, FFE:]).astype(jnp.bfloat16)
-    returned = lax.all_to_all(
+    returned = jnp.concatenate(
         lax.all_to_all(
-            jnp.dot(hidden, w_down[0], preferred_element_type=jnp.float32)
-            .astype(jnp.bfloat16)
-            .reshape(arrived.shape),
-            "seq",
-            split_axis=0,
-            concat_axis=0,
-            tiled=True,
+            jnp.stack(
+                jnp.split(
+                    lax.all_to_all(
+                        jnp.dot(hidden, w_down[0], preferred_element_type=jnp.float32)
+                        .astype(jnp.bfloat16)
+                        .reshape(arrived.shape),
+                        "seq",
+                        split_axis=0,
+                        concat_axis=0,
+                        tiled=True,
+                    ),
+                    lax.axis_size("exp"),
+                    axis=1,
+                )
+            ),
+            "exp",
+            0,
+            0,
         ),
-        "exp",
-        split_axis=1,
-        concat_axis=1,
-        tiled=True,
+        axis=1,
     )
     picked = returned.reshape(-1, width)[target].astype(jnp.float32).reshape(rows, TOP, width)
     moe = jnp.sum(expert_scale[..., None] * picked, axis=1)

time: 602 us -> 620 us (1.030)
  local copies, waits for them, and re-layouts: 46.5 us -> 64.2 us
    unnamed x21 -> x52, local copies, waits for them, and re-layouts: 1.46 us -> 22 us
    all_to_all x2 -> x0, local copies, waits for them, and re-layouts: 8.18 us -> none  [the longest x1 4.61 us: local(): lax.all_to_all(lax.all_to_all(jnp.dot(hidden, w_down[0], preferred_elemen...]
where the time goes in v1:
time: 620 us; the launch traced here: 617 us
  waiting for transfers between devices  278 us (45%)
  blocking collectives  120 us (19%)
  local copies, waits for them, and re-layouts  64.2 us (10%)
  other arithmetic  59.3 us (10%)
  matrix products  52.6 us (8%)
  starting transfers between devices  28.3 us (5%)
  between operations  13.8 us (2%)
    reduce_scatter x1, waiting for transfers between devices, local(): lax.psum_scatter(jnp.dot(gated, out_weight, preferred_element_type=jnp.fl...  222 us
    all_to_all x1, blocking collectives, local(): lax.all_to_all(lax.all_to_all(outgoing, 'seq', split_axis=0, concat_axis=...  57.9 us
    all_to_all x1, waiting for transfers between devices, local(): lax.all_to_all(jnp.stack(jnp.split(lax.all_to_all(jnp.dot(hidden, w_down[...  49.5 us
    dot_general x59, matrix products, contract(): return jnp.einsum(form, left, right, precision=lax.Precision.HIGHEST)  41.1 us
    another operation x4, other arithmetic, local(): lax.linalg.triangular_solve(system, right, left_side=True, lower=True, un...  39.4 us
    all_to_all x1, blocking collectives, local(): lax.all_to_all(outgoing, 'seq', split_axis=0, concat_axis=0, tiled=True)  31.5 us
    all_to_all x1, blocking collectives, local(): lax.all_to_all(jnp.dot(hidden, w_down[0], preferred_element_type=jnp.floa...  30.7 us
    ppermute x7, starting transfers between devices, passed_along(): return lax.ppermute(array, axis, pairs)  22.7 us
  transfers between devices with their start and end apart: 9, of which 9 were waited for; matrix products, arithmetic and copies ran while one was open for 0% of the time, Pallas kernels for 0%

profile of v1, /device:TPU:4, one launch (start us, length us, event | category | flops | bytes accessed | tf_op | source)
XLA Modules:
  0.0 616.7 jit_solution(3993847111385925343)
XLA Ops:
  14.5 39.3 %custom-call.3 = f32[1,8,1,64,64]{3,4,2,1,0:T(8,128)S(1)} custom-call(f32[1,8,1,64,64]{4,3,2,1,0:T(8,128)S(1)} %fusion.44), custom_call_target="InvertDiagBlocksLowerTriangular" | custom-call | tf_op jit(solution)/shard_map/triangular_solve | solution.py:80
  58.3 5.2 while.34
  65.7 42.1 %while.35 = (s32[]{:T(128)}, f32[1,128,128]{2,1,0:T(8,128)S(1)}, pred[]{:T(512)}, f32[1,128,128]{2,1,0:T(8,128)}, f32[1,128,128]{2,1,0:T(8,128)}, /*index=5*/f32[1,128,128]{2,1,0:T(8,128)}, s32[]{:T(128)}) while((s32[]{:T(128)}, f32[1,128,128]{2,1,0:T(8,128)S(1)}, pred[]{:T(512)}, f32[1,128,128]{2,1,0:T(8,128)}, f32[1,128,128]{2,1,0:T(8,128)}, ...), condition=%wide.region_6.7_spmd, body=%wide.region_5.6_spmd.sunk | while | flops 25231360 | bytes 524406 | solution.py:109
  77.2 3.6 collective-permute-start
  83.5 3.6 collective-permute-start
  89.9 3.6 collective-permute-start
  96.2 3.6 collective-permute-start
  102.6 3.6 collective-permute-start
  110.9 24.3 %while.36 = (s32[]{:T(128)}, f32[1,128,128]{1,2,0:T(8,128)S(1)}, f32[8,1,64,128]{3,2,1,0:T(8,128)}, f32[8,1,128,128]{3,2,1,0:T(8,128)S(1)}, f32[8,1,128,128]{2,3...) while((s32[]{:T(128)}, f32[1,128,128]{1,2,0:T(8,128)S(1)}, ...), condition=%wide.region_8.9_spmd, body=%wide.region_7.8_spmd.sunk | while | flops 56664064 | bytes 823413 | solution.py:121
  141.7 222.1 %reduce-scatter.2.cloned.1.call-done = bf16[16,2048]{1,0:T(8,128)(2,1)} async-done(((bf16[512,2048]{1,0:T(8,128)(2,1)}), bf16[16,2048]{1,0:T(8,128)(2,1)}) %reduce-scatter.2.cloned.1.call-update) | async-done | bytes 65552 | tf_op jit(solution)/shard_map/reduce_scatter | solution.py:132
  366.9 3.8 scatter_custom_fusion
  370.7 4.4 reshape.481
  375.1 31.5 %all_to_all.20 = bf16[8,32,2,2048]{3,2,1,0:T(2,128)(2,1)S(1)} all-to-all(bf16[8,32,2,2048]{3,2,1,0:T(2,128)(2,1)} %reshape.481), channel_id=1, replica_groups=mesh['seq'=8,'exp'=32] {'seq'}, dimensions={0} | all-to-all | bytes 4194304 | tf_op jit(solution)/shard_map/all_to_all | solution.py:155
  408.9 57.9 %all_to_all.21 = bf16[8,32,2,2048]{3,2,0,1:T(2,128)(2,1)S(1)} all-to-all(bf16[8,32,2,2048]{3,2,0,1:T(2,128)(2,1)S(1)} %copy.171), channel_id=1, replica_groups=mesh['seq'=8,'exp'=32] {'exp'}, dimensions={1} | all-to-all | bytes 4194304 | tf_op jit(solution)/shard_map/all_to_all | solution.py:154
  466.8 3.1 copy.172
  469.9 4.1 reshape.482
  474.0 5.1 fusion.34
  481.8 4.4 reshape.483
  486.2 30.7 %all_to_all.22 = bf16[8,32,2,2048]{3,2,1,0:T(2,128)(2,1)S(1)} all-to-all(bf16[8,32,2,2048]{3,2,1,0:T(2,128)(2,1)} %reshape.483), channel_id=1, replica_groups=mesh['seq'=8,'exp'=32] {'seq'}, dimensions={0} | all-to-all | bytes 4194304 | tf_op jit(solution)/shard_map/all_to_all | solution.py:168
  538.2 5.6 all-to-all-start.3
  543.8 49.5 %all-to-all-done.3 = bf16[32,8,1,2,2048]{4,3,1,2,0:T(2,128)(2,1)} async-done(((bf16[32,8,1,2,2048]{4,3,1,2,0:T(2,128)(2,1)}), bf16[32,8,1,2,2048]{4,3,1,2,0:T(2,128)(2,1)}, u32[]{:S(2)}, u32[]{:S(2)}) %all-to-all-start.3) | async-done | bytes 2097184 | tf_op jit(solution)/shard_map/all_to_all | solution.py:165
  593.3 4.6 copy.204
  598.0 4.1 reshape_reshape.3
  602.1 3.5 gather_fusion
  (224 shorter events, 110.2 us)
Async XLA Ops:
  6.5 472.6 %copy-start = (bf16[1,512,2048]{2,1,0:T(8,128)(2,1)S(1)}, bf16[1,512,2048]{2,1,0:T(8,128)(2,1)}, u32[]{:S(2)}) copy-start(bf16[1,512,2048]{2,1,0:T(8,128)(2,1)} %param.37) | copy-start | bytes 6291460
  6.5 47.6 %copy-start.3 = (bf16[512,128]{1,0:T(8,128)(2,1)S(1)}, bf16[512,128]{1,0:T(8,128)(2,1)}, u32[]{:S(2)}) copy-start(bf16[512,128]{1,0:T(8,128)(2,1)} %param.24) | copy-start | bytes 393220
  6.5 357.3 %reduce-scatter.2.cloned.1.call-start = ((), (), s32[]{:S(2)}) async-start(), calls=%async_computation.5 | async-start | bytes 2162688 | tf_op jit(solution)/shard_map/reduce_scatter | solution.py:132
  12.1 43.8 %copy-start.7 = (pred[64,64]{1,0:T(8,128)(4,1)}, pred[64,64]{1,0:T(8,128)(4,1)S(1)}, u32[]{:S(2)}) copy-start(pred[64,64]{1,0:T(8,128)(4,1)S(1)} %get-tuple-element.253) | copy-start | bytes 12292
  66.8 2.6 collective-permute-start
  71.3 4.0 collective-permute-start
  77.2 4.4 collective-permute-start
  83.5 4.4 collective-permute-start
  89.9 4.4 collective-permute-start
  96.2 4.4 collective-permute-start
  102.6 4.4 collective-permute-start
  110.9 25.5 %copy-start.8 = (f32[128]{0:T(128)S(1)}, f32[128]{0:T(128)}, u32[]{:S(2)}) copy-start(f32[128]{0:T(128)} %param.30) | copy-start | bytes 1540
  137.6 3.1 copy-start.4
  140.7 223.1 %copy-start.1 = (bf16[16,2048]{1,0:T(8,128)(2,1)S(1)}, bf16[16,2048]{1,0:T(8,128)(2,1)}, u32[]{:S(2)}) copy-start(bf16[16,2048]{1,0:T(8,128)(2,1)} %param.32) | copy-start | bytes 196612
  140.7 224.0 %copy-start.6 = (f32[2048]{0:T(1024)S(1)}, f32[2048]{0:T(1024)}, u32[]{:S(2)}) copy-start(f32[2048]{0:T(1024)} %param.33) | copy-start | bytes 24580
  538.2 55.2 %all-to-all-start.3 = ((bf16[32,8,1,2,2048]{4,3,1,2,0:T(2,128)(2,1)}), bf16[32,8,1,2,2048]{4,3,1,2,0:T(2,128)(2,1)}, u32[]{:S(2)}, u32[]{:S(2)}) async-start(bf16[32,8,1,2,2048]{4,3,1,2,0:T(2,128)(2,1)} %fusion.82), calls=%async_computation.4 | async-start | bytes 4194304 | tf_op jit(solution)/shard_map/all_to_all | solution.py:165
  605.6 1.5 copy-start.5
  605.6 3.6 copy-start.2
Sparse Core Ops, SparseCore 0:
  140.9 222.8 reduce-scatter.1
